TPU v7x, 32 devices: a whole 2x2x4 slice. The times are simulated.
32 devices in a mesh: rep: 8 (over y, x, core), shard: 4 (over z).
Axes of the slice: x: 2, y: 2, z: 4, core: 2. Of those that a mesh axis runs over, the one named last changes fastest.
Arguments:
- layer_input: bfloat16 [16384, 2048], P(('rep', 'shard')), may hold values from -6 to 6
- gain_attn: bfloat16 [2048], P('shard'), may hold values from 0.5 to 1.5
- w_query: bfloat16 [2048, 2048], P('shard'), may hold values from -0.125 to 0.125
- w_key: bfloat16 [2048, 2048], P('shard'), may hold values from -0.125 to 0.125
- w_value: bfloat16 [2048, 2048], P('shard'), may hold values from -0.125 to 0.125
- w_out: bfloat16 [2048, 2048], P(None, 'shard'), may hold values from -0.5 to 0.5
- gain_mlp: bfloat16 [2048], P('shard'), may hold values from 0.5 to 1.5
- w_gate: bfloat16 [2048, 5632], P('shard'), may hold values from -0.125 to 0.125
- w_up: bfloat16 [2048, 5632], P('shard'), may hold values from -0.125 to 0.125
- w_down: bfloat16 [5632, 2048], P(None, 'shard'), may hold values from -0.078125 to 0.078125
- segments: int32 [32, 512], P(('rep', 'shard')), may hold values from 0 to 3, never falling along the last dimension, each value on 1 to 256 neighbouring positions
- attn_route: int32 [16384, 2], P(('rep', 'shard')), may hold values from 0 to 7, all different within a row
- attn_gate: float32 [16384, 2], P(('rep', 'shard')), may hold values from 0.2 to 1
- mlp_route: int32 [16384, 2], P(('rep', 'shard')), may hold values from 0 to 7, all different within a row
- mlp_gate: float32 [16384, 2], P(('rep', 'shard')), may hold values from 0.2 to 1
- cotangent: bfloat16 [16384, 2048], P(('rep', 'shard')), may hold values from -6 to 6
Outputs:
- output: bfloat16 [16384, 2048], P(('rep', 'shard'))
- grad_input: bfloat16 [16384, 2048], P(('rep', 'shard'))
- grad_gain_attn: float32 [2048], P('shard')
- grad_query: float32 [2048, 2048], P('shard')
- grad_key: float32 [2048, 2048], P('shard')
- grad_value: float32 [2048, 2048], P('shard')
- grad_out: float32 [2048, 2048], P(None, 'shard')
- grad_gain_mlp: float32 [2048], P('shard')
- grad_gate: float32 [2048, 5632], P('shard')
- grad_up: float32 [2048, 5632], P('shard')
- grad_down: float32 [5632, 2048], P(None, 'shard')
All inputs are finite; a program needn't handle non-finite values.
Results may differ from a plain program's by a relative error of at most 0.017.
Values may be sent and summed in bfloat16 or wider, within the bound.
A program may use at most 384 MiB of HBM per device.

v0:
```python
import jax
import jax.numpy as jnp
from jax import lax
from jax.sharding import PartitionSpec as P

HEADS = 16
HD = 128
WIN = 256
CAP = 128
EPSILON = 1e-05
BF = jnp.bfloat16
F32 = jnp.float32


def mm(left, right):
    return jnp.dot(left, right, preferred_element_type=F32)


def mm_nt(left, right):
    return lax.dot_general(left, right, (((1,), (1,)), ((), ())), preferred_element_type=F32)


def mm_tn(left, right):
    return lax.dot_general(left, right, (((0,), (0,)), ((), ())), preferred_element_type=F32)


def swap(value, bit):
    size = lax.axis_size("rep")
    return lax.ppermute(value, "rep", [(i, i ^ bit) for i in range(size)])


def chip_bits():
    size, bits, bit = (lax.axis_size("rep"), [], 2)
    while bit < size:
        bits.append(bit)
        bit *= 2
    return bits


def chip_offsets():
    return list(range(0, lax.axis_size("rep"), 2))


def gather_chips(value):
    bits = chip_bits()
    if len(bits) == 2:
        one, two = bits
        half = value.shape[0] // 2
        by_one, by_two = (swap(value, one), swap(value, two))
        far = jnp.concatenate([swap(by_one[:half], two), swap(by_two[half:], one)], axis=0)
        return {0: value, one: by_one, two: by_two, one ^ two: far}
    blocks = {0: value}
    for bit in bits:
        blocks.update({d ^ bit: swap(b, bit) for d, b in list(blocks.items())})
    return blocks


def add(left, right):
    return left.astype(F32) + right.astype(F32)


def scatter_chips(blocks):
    bits = chip_bits()
    if len(bits) == 2:
        one, two = bits
        half = blocks[0].shape[0] // 2
        far = blocks[one ^ two]
        near_one, near_two = (blocks[one], blocks[two])
        top, bottom = (swap(far[:half], one), swap(far[half:], two))
        two_bottom, one_top = (swap(near_two[half:], two), swap(near_one[:half], one))
        two_top = swap(add(near_two[:half], top).astype(BF), two)
        one_bottom = swap(add(near_one[half:], bottom).astype(BF), one)
        by_one = jnp.concatenate([one_top, one_bottom], axis=0)
        by_two = jnp.concatenate([two_top, two_bottom], axis=0)
        return blocks[0].astype(F32) + by_one.astype(F32) + by_two.astype(F32)
    blocks = dict(blocks)
    for bit in reversed(bits):
        kept = {d: b for d, b in blocks.items() if not d & bit}
        blocks = {d: add(b, swap(blocks[d | bit], bit)).astype(BF) for d, b in kept.items()}
    return blocks[0].astype(F32)


def gather_plane(value):
    blocks = gather_chips(value)
    same = jnp.concatenate([blocks[d] for d in chip_offsets()], axis=0)
    return jnp.concatenate([same, swap(same, 1)], axis=0)


def scatter_plane(partial):
    half = partial.shape[0] // 2
    same = add(partial[:half], swap(partial[half:], 1)).astype(BF)
    offsets = chip_offsets()
    rows = half // len(offsets)
    return scatter_chips({d: same[i * rows : (i + 1) * rows] for i, d in enumerate(offsets)})


def rotary_tables(length):
    half = HD // 2
    positions = jnp.arange(length, dtype=F32)
    inverse = 10000.0 ** (-2.0 * jnp.arange(half, dtype=F32) / HD)
    angles = positions[:, None] * inverse[None, :]
    return (jnp.cos(angles)[:, None, :], jnp.sin(angles)[:, None, :])


def rotate(values, cos_table, sin_table):
    half = values.shape[-1] // 2
    first, second = (values[..., :half], values[..., half:])
    return jnp.concatenate(
        [first * cos_table - second * sin_table, second * cos_table + first * sin_table], axis=-1
    )


def plan_slots(route_ids, gate_values):
    hit_mask = route_ids == 0
    hit = jnp.any(hit_mask, axis=-1)
    weight = jnp.sum(jnp.where(hit_mask, gate_values, 0.0), axis=-1)
    ids = jnp.arange(route_ids.shape[0], dtype=jnp.int32)
    earlier = (ids[None, :] < ids[:, None]) & hit[None, :]
    order = jnp.sum(earlier.astype(jnp.int32), axis=1)
    kept = hit & (order < CAP)
    slots = jnp.arange(CAP, dtype=jnp.int32)
    table = (order[None, :] == slots[:, None]) & kept[None, :]
    return (table, jnp.where(kept, weight, 0.0))


def norm_back(grad_normed, source, root, gain):
    scaled = grad_normed * gain
    grad_gain = jnp.sum(grad_normed * source * root, axis=0)
    mean = jnp.mean(scaled * source, axis=-1, keepdims=True)
    return (grad_gain, root * scaled - source * (root * root * root) * mean)


def gather_vector(rows):
    size, me = (lax.axis_size("shard"), lax.axis_index("shard"))
    parts = [rows] + [
        lax.ppermute(rows, "shard", [(i, (i - k) % size) for i in range(size)])
        for k in range(1, size)
    ]
    twice = jnp.concatenate(parts + parts, axis=1)
    own = rows.shape[1]
    return lax.dynamic_slice_in_dim(twice, (size - me) % size * own, size * own, 1)


def attend(qkv, tables, allowed):
    rows = qkv.shape[0]
    length = allowed.shape[-1]
    seqs = rows // length
    width = qkv.shape[1] // 3
    heads = width // HD
    shape = (seqs, length, heads, HD)
    queries = rotate(qkv[:, :width].reshape(shape), *tables).astype(BF)
    keys = rotate(qkv[:, width : 2 * width].reshape(shape), *tables).astype(BF)
    values = qkv[:, 2 * width :].astype(BF).reshape(shape)
    scores = jnp.einsum("bqhd,bkhd->bhqk", queries, keys, preferred_element_type=F32) * HD ** (-0.5)
    scores = jnp.where(allowed[:, None], scores, -1e30)
    peak = jnp.max(scores, axis=-1, keepdims=True)
    raw = jnp.exp(scores - peak)
    total = jnp.sum(raw, axis=-1, keepdims=True)
    probs = (raw / total).astype(BF)
    context = jnp.einsum("bhqk,bkhd->bqhd", probs, values, preferred_element_type=F32).astype(BF)
    return (context.reshape(rows, width), (queries, keys, values, peak + jnp.log(total)))


def attend_back(saved, grad_context, tables, allowed):
    queries, keys, values, lse = saved
    shape = queries.shape
    grad_context = grad_context.reshape(shape)
    scale = HD ** (-0.5)
    scores = jnp.einsum("bqhd,bkhd->bhqk", queries, keys, preferred_element_type=F32) * scale
    scores = jnp.where(allowed[:, None], scores, -1e30)
    probs = jnp.exp(scores - lse)
    grad_values = jnp.einsum(
        "bhqk,bqhd->bkhd", probs.astype(BF), grad_context, preferred_element_type=F32
    ).astype(BF)
    grad_probs = jnp.einsum("bqhd,bkhd->bhqk", grad_context, values, preferred_element_type=F32)
    inner = jnp.sum(probs * grad_probs, axis=-1, keepdims=True)
    grad_scores = (probs * (grad_probs - inner)).astype(BF)
    grad_queries = (
        jnp.einsum("bhqk,bkhd->bqhd", grad_scores, keys, preferred_element_type=F32) * scale
    )
    grad_keys = (
        jnp.einsum("bhqk,bqhd->bkhd", grad_scores, queries, preferred_element_type=F32) * scale
    )
    cos_table, sin_table = tables
    rows = shape[0] * shape[1]
    return jnp.concatenate(
        [
            rotate(grad_queries, cos_table, -sin_table).astype(BF).reshape(rows, -1),
            rotate(grad_keys, cos_table, -sin_table).astype(BF).reshape(rows, -1),
            grad_values.reshape(rows, -1),
        ],
        axis=1,
    )


def per_device(
    layer_input,
    gain_attn,
    w_query,
    w_key,
    w_value,
    w_out,
    gain_mlp,
    w_gate,
    w_up,
    w_down,
    segments,
    attn_route,
    attn_gate,
    mlp_route,
    mlp_gate,
    cotangent,
):
    length = layer_input.shape[0]
    size = lax.axis_size("rep")
    me = lax.axis_index("rep")
    block = w_query.shape[1] // size
    hidden_block = w_gate.shape[1] // size
    offsets = chip_offsets()

    def columns(weight, width):
        return lax.dynamic_slice_in_dim(weight, me * width, width, 1)

    def rows_of(weight, height):
        return lax.dynamic_slice_in_dim(weight, me * height, height, 0)

    own_qkv = jnp.concatenate([columns(w, block) for w in (w_query, w_key, w_value)], axis=1)
    own_qkv = lax.all_gather(own_qkv, "shard", axis=0, tiled=True)
    own_out = lax.all_gather(rows_of(w_out, block), "shard", axis=1, tiled=True)
    qkv_w = gather_chips(own_qkv)
    out_w = gather_chips(own_out)
    gate_up = jnp.concatenate([columns(w_gate, hidden_block), columns(w_up, hidden_block)], axis=1)
    gate_up = lax.all_gather(gate_up, "shard", axis=0, tiled=True)
    down = lax.all_gather(rows_of(w_down, hidden_block), "shard", axis=1, tiled=True)
    gains = gather_vector(jnp.stack([gain_attn, gain_mlp])).astype(F32)
    gain_one, gain_two = (gains[0], gains[1])
    table, mix = plan_slots(mlp_route, mlp_gate)
    pick = table.astype(BF)
    upstream = cotangent.astype(F32)
    slot_weight = jnp.sum(jnp.where(table, mix[None, :], 0.0), axis=1)[:, None]
    slot_grad = (mm(pick, cotangent) * slot_weight).astype(BF)
    all_slot_grad = gather_plane(slot_grad)
    inputs = layer_input.astype(F32)
    root_one = lax.rsqrt(jnp.mean(inputs * inputs, axis=-1, keepdims=True) + EPSILON)
    normed = (inputs * root_one * gain_one).astype(BF)
    both = jnp.concatenate([normed, swap(normed, 1)], axis=0)
    seg = jnp.concatenate([segments, swap(segments, 1)], axis=0)
    ids = jnp.arange(length, dtype=jnp.int32)
    distance = ids[:, None] - ids[None, :]
    near = (distance >= 0) & (distance < WIN)
    allowed = (seg[:, :, None] == seg[:, None, :]) & near[None]
    tables = rotary_tables(length)
    context, saved = ({}, {})
    for d in offsets:
        context[d], saved[d] = attend(mm(both, qkv_w[d]), tables, allowed)
    all_context = jnp.concatenate([context[d] for d in offsets], axis=1)
    all_out = jnp.concatenate([out_w[d] for d in offsets], axis=0)
    projected = mm(all_context, all_out)
    projected = projected[:length] + swap(projected[length:].astype(BF), 1).astype(F32)
    attn_weight = jnp.sum(jnp.where(attn_route == 0, attn_gate, 0.0), axis=-1)[:, None]
    hidden = inputs + projected * attn_weight
    root_two = lax.rsqrt(jnp.mean(hidden * hidden, axis=-1, keepdims=True) + EPSILON)
    normed_two = (hidden * root_two * gain_two).astype(BF)
    dispatched = gather_plane(mm(pick, normed_two).astype(BF))
    act = mm(dispatched, gate_up)
    gate_act, up_act = (act[:, :hidden_block], act[:, hidden_block:])
    sigmoid = jax.nn.sigmoid(gate_act)
    silu = gate_act * sigmoid
    inner = (silu * up_act).astype(BF)
    grad_inner = mm_nt(all_slot_grad, down)
    grad_gate_act = (grad_inner * up_act * sigmoid * (1.0 + gate_act * (1.0 - sigmoid))).astype(BF)
    grad_up_act = (grad_inner * silu).astype(BF)
    grad_act = jnp.concatenate([grad_gate_act, grad_up_act], axis=1)
    grad_disp = scatter_plane(mm_nt(grad_act, gate_up).astype(BF)).astype(BF)
    expert_out = scatter_plane(mm(inner, down).astype(BF)).astype(BF)
    output = (hidden + mm_tn(pick, expert_out) * mix[:, None]).astype(BF)
    grad_gate_up = mm_tn(dispatched, grad_act).astype(BF)
    grad_down = mm_tn(inner, all_slot_grad).astype(BF)
    grad_normed_two = mm_tn(pick, grad_disp)
    grad_gain_two, through = norm_back(grad_normed_two, hidden, root_two, gain_two)
    grad_hidden = upstream + through
    grad_projected = (grad_hidden * attn_weight).astype(BF)
    both_grad = jnp.concatenate([grad_projected, swap(grad_projected, 1)], axis=0)
    grad_out_w = mm_tn(all_context, both_grad).astype(BF)
    grad_context = mm_nt(both_grad, all_out).astype(BF)
    grad_lin = {
        d: attend_back(saved[d], grad_context[:, i * block : (i + 1) * block], tables, allowed)
        for i, d in enumerate(offsets)
    }
    grad_qkv_w = {d: mm_tn(both, grad_lin[d]).astype(BF) for d in offsets}
    grad_normed = sum((mm_nt(grad_lin[d], qkv_w[d]) for d in offsets))
    grad_normed = grad_normed[:length] + swap(grad_normed[length:].astype(BF), 1).astype(F32)
    grad_gain_one, first = norm_back(grad_normed, inputs, root_one, gain_one)
    grad_input = (grad_hidden + first).astype(BF)

    def spread(value, axis):
        return lax.all_gather(value, "rep", axis=axis, tiled=True).astype(F32)

    sum_gu = lax.psum_scatter(grad_gate_up, "shard", scatter_dimension=0, tiled=True)
    sum_down = lax.psum_scatter(grad_down, "shard", scatter_dimension=1, tiled=True)
    own_grad_out = scatter_chips(
        {d: grad_out_w[i * block : (i + 1) * block] for i, d in enumerate(offsets)}
    ).astype(BF)
    sum_out = lax.psum_scatter(own_grad_out, "shard", scatter_dimension=1, tiled=True)
    own_grad_qkv = scatter_chips(grad_qkv_w).astype(BF)
    sum_qkv = lax.psum_scatter(own_grad_qkv, "shard", scatter_dimension=0, tiled=True)
    grad_gate = spread(sum_gu[:, :hidden_block], 1)
    grad_up = spread(sum_gu[:, hidden_block:], 1)
    grad_down = spread(sum_down, 0)
    grad_out = spread(sum_out, 0)
    grad_query, grad_key, grad_value = (
        spread(sum_qkv[:, i * block : (i + 1) * block], 1) for i in range(3)
    )
    gain_grads = lax.psum(jnp.stack([grad_gain_one, grad_gain_two]), ("rep", "shard"))
    own = gain_attn.shape[0]
    gain_grads = lax.dynamic_slice_in_dim(gain_grads, lax.axis_index("shard") * own, own, 1)
    return (
        output,
        grad_input,
        gain_grads[0],
        grad_query,
        grad_key,
        grad_value,
        grad_out,
        gain_grads[1],
        grad_gate,
        grad_up,
        grad_down,
    )


def solution(mesh):
    tokens = P(("rep", "shard"), None)
    tall, wide, vector = (P("shard", None), P(None, "shard"), P("shard"))
    weights = (vector, tall, tall, tall, wide, vector, tall, tall, wide)
    return jax.shard_map(
        per_device,
        mesh=mesh,
        in_specs=(tokens, *weights) + (tokens,) * 6,
        out_specs=(tokens, tokens, *weights),
        check_vma=False,
    )
```

profile of v0, /device:TPU:0, one launch (start us, length us, event | category | flops | bytes accessed | tf_op | source)
XLA Modules:
  0.0 1188.0 jit_solution(6927684167405556137)
XLA Ops:
  25.8 15.1 %all-gather.14.cloned.1.call-done = bf16[256,2048]{1,0:T(8,128)(2,1)} async-done(((bf16[256,512]{1,0:T(8,128)(2,1)}), bf16[256,2048]{1,0:T(8,128)(2,1)}) %all-gather.14.cloned.1.call-update) | async-done | bytes 1048592 | tf_op jit(solution)/shard_map/all_gather | solution.py:229
  48.7 57.4 %all-gather.12.cloned.1.call-done = bf16[2048,768]{1,0:T(8,128)(2,1)} async-done(((bf16[512,768]{1,0:T(8,128)(2,1)}), bf16[2048,768]{1,0:T(8,128)(2,1)}) %all-gather.12.cloned.1.call-update) | async-done | bytes 3145744 | tf_op jit(solution)/shard_map/all_gather | solution.py:228
  124.0 63.3 %collective-permute-done.12 = bf16[128,2048]{1,0:T(8,128)(2,1)S(1)} collective-permute-done((bf16[128,2048]{1,0:T(8,128)(2,1)S(1)}, bf16[128,2048]{1,0:T(8,128)(2,1)S(1)}, u32[]{:S(2)}, u32[]{:S(2)}) %collective-permute-start.12) | collective-permute-done | bytes 524320 | tf_op jit(solution)/shard_map/ppermute | solution.py:29
  221.0 8.6 fusion.149
  342.6 11.5 collective-permute-done.26
  364.9 8.4 collective-permute-done.14
  389.3 12.3 %fusion.178 = f32[1024,1408]{1,0:T(8,128)} fusion(bf16[1024,2048]{1,0:T(8,128)(2,1)} %constant_dynamic-update-slice_fusion.20, bf16[2048,1408]{1,0:T(8,128)(2,1)} %all-gather.16.cloned.1.call-done), kind=kOutput, calls=%fused_computation.378 | convolution fusion | flops 5905580032 | bytes 15728640 | tf_op jit(solution)/shard_map/dot_general | solution.py:16
  401.6 40.2 %all-gather.18.cloned.1.call-done = bf16[704,2048]{1,0:T(8,128)(2,1)} async-done(((bf16[704,512]{1,0:T(8,128)(2,1)}), bf16[704,2048]{1,0:T(8,128)(2,1)}) %all-gather.18.cloned.1.call-update) | async-done | bytes 2883600 | tf_op jit(solution)/shard_map/all_gather | solution.py:234
  441.8 10.3 multiply_convert_fusion.7
  505.1 10.7 collective-permute-done.49
  527.7 9.9 collective-permute-done.48
  539.5 7.6 convolution_convert_fusion.8
  626.2 8.0 convolution_convert_fusion.6
  650.6 10.1 collective-permute-done.41
  673.1 22.7 %collective-permute-done.40 = bf16[1024,768]{1,0:T(8,128)(2,1)} collective-permute-done((bf16[1024,768]{1,0:T(8,128)(2,1)}, bf16[1024,768]{1,0:T(8,128)(2,1)}, u32[]{:S(2)}, u32[]{:S(2)}) %collective-permute-start.40) | collective-permute-done | bytes 1572896 | tf_op jit(solution)/shard_map/ppermute | solution.py:29
  695.8 31.6 %collective-permute-done.42 = bf16[1024,768]{1,0:T(8,128)(2,1)} collective-permute-done((bf16[1024,768]{1,0:T(8,128)(2,1)}, bf16[1024,768]{1,0:T(8,128)(2,1)}, u32[]{:S(2)}, u32[]{:S(2)}) %collective-permute-start.42) | collective-permute-done | bytes 1572896 | tf_op jit(solution)/shard_map/ppermute | solution.py:29
  727.4 9.3 add_convert_fusion
  736.9 10.9 convolution_convert_fusion
  749.2 46.1 %reduce-scatter.5.cloned.1.call-done = bf16[512,768]{1,0:T(8,128)(2,1)} async-done(((bf16[2048,768]{1,0:T(8,128)(2,1)}), bf16[512,768]{1,0:T(8,128)(2,1)}) %reduce-scatter.5.cloned.1.call-update) | async-done | bytes 786448 | tf_op jit(solution)/shard_map/reduce_scatter | solution.py:306
  798.7 101.9 %reduce-scatter.9.cloned.1.call-done = bf16[512,1408]{1,0:T(8,128)(2,1)} async-done(((bf16[2048,1408]{1,0:T(8,128)(2,1)}), bf16[512,1408]{1,0:T(8,128)(2,1)}) %reduce-scatter.9.cloned.1.call-update) | async-done | bytes 1441808 | tf_op jit(solution)/shard_map/reduce_scatter | solution.py:299
  914.4 7.8 fusion.181
  922.2 7.7 fusion.179
  929.9 7.7 fusion.180
  937.6 11.8 add_add_fusion
  962.2 10.7 collective-permute-done.23
  1000.2 39.9 %psum.7 = f32[2,2048]{1,0:T(2,128)S(1)} all-reduce(f32[2,2048]{1,0:T(2,128)S(1)} %pad_maximum_fusion.43), channel_id=1, replica_groups=mesh['rep'=8,'shard'=4] {'rep','shard'}, use_global_device_ids=true, to_apply=%region_23.24 | all-reduce | flops 4096 | bytes 32768 | tf_op jit(solution)/shard_map/psum | solution.py:314
  1051.2 8.7 convert_element_type.490
  1068.2 13.3 %all-gather.24.cloned.1.call-done = bf16[512,2048]{1,0:T(8,128)(2,1)} async-done(((bf16[512,256]{1,0:T(8,128)(2,1)}), bf16[512,2048]{1,0:T(8,128)(2,1)}) %all-gather.24.cloned.1.call-update) | async-done | bytes 2097168 | tf_op jit(solution)/shard_map/all_gather | solution.py:297
  1085.6 41.1 %all-gather.28.cloned.1.call-done = bf16[512,5632]{0,1:T(8,128)(2,1)} async-done(((bf16[512,704]{0,1:T(8,128)(2,1)}), bf16[512,5632]{0,1:T(8,128)(2,1)}) %all-gather.28.cloned.1.call-update) | async-done | bytes 5767184 | tf_op jit(solution)/shard_map/all_gather | solution.py:297
  1126.8 9.1 copy.333
  1135.8 36.2 %all-gather.30.cloned.1.call-done = bf16[512,5632]{0,1:T(8,128)(2,1)} async-done(((bf16[512,704]{0,1:T(8,128)(2,1)}), bf16[512,5632]{0,1:T(8,128)(2,1)}) %all-gather.30.cloned.1.call-update) | async-done | bytes 5767184 | tf_op jit(solution)/shard_map/all_gather | solution.py:297
  1172.0 9.2 copy.334
  (633 shorter events, 472.7 us)
Async XLA Ops:
  7.2 33.6 %all-gather.14.cloned.1.call-start = ((), (), s32[]{:S(2)}) async-start(), calls=%async_computation.5 | async-start | bytes 1310720 | tf_op jit(solution)/shard_map/all_gather | solution.py:229
  9.5 96.5 %all-gather.12.cloned.1.call-start = ((), (), s32[]{:S(2)}) async-start(), calls=%async_computation.4 | async-start | bytes 3932160 | tf_op jit(solution)/shard_map/all_gather | solution.py:228
  12.7 376.6 %all-gather.16.cloned.1.call-start = ((), (), s32[]{:S(2)}) async-start(), calls=%async_computation.6 | async-start | bytes 7208960 | tf_op jit(solution)/shard_map/all_gather | solution.py:233
  18.9 88.6 %collective-permute-start.4 = (s32[1,512]{1,0:T(1,128)S(1)}, s32[1,512]{1,0:T(1,128)S(1)}, u32[]{:S(2)}, u32[]{:S(2)}) collective-permute-start(s32[1,512]{1,0:T(1,128)S(1)} %copy-done.131), channel_id=1, source_target_pairs={{0,4},{4,0},{8,12},{12,8},{16,20},{20,16},{24,28},{28,24},{1,5},{5... | collective-permute-start | bytes 6152 | tf_op jit(solution)/shard_map/ppermute | solution.py:29
  25.4 164.0 %collective-permute-start.3 = (bf16[512,2048]{1,0:T(8,128)(2,1)}, bf16[512,2048]{1,0:T(8,128)(2,1)}, u32[]{:S(2)}, u32[]{:S(2)}) collective-permute-start(bf16[512,2048]{1,0:T(8,128)(2,1)} %fusion.2), channel_id=1, source_target_pairs={{0,4},{4,0},{8,12},{12,8},{16,20},{20,16},{24,28},{28,24},{1,5},{5... | collective-permute-start | bytes 6291464 | tf_op jit(solution)/shard_map/ppermute | solution.py:29
  40.9 67.1 %collective-permute-start.9 = (bf16[256,2048]{1,0:T(8,128)(2,1)}, bf16[256,2048]{1,0:T(8,128)(2,1)}, u32[]{:S(2)}, u32[]{:S(2)}) collective-permute-start(bf16[256,2048]{1,0:T(8,128)(2,1)} %all-gather.14.cloned.1.call-done), channel_id=1, source_target_pairs={{0,8},{4,12},{8,0},{12,4},{16,24},{20,28},{24,16},{28,20},{1,9},{5... | collective-permute-start | bytes 3145736 | tf_op jit(solution)/shard_map/ppermute | solution.py:29
  45.0 396.7 %all-gather.18.cloned.1.call-start = ((), (), s32[]{:S(2)}) async-start(), calls=%async_computation.7 | async-start | bytes 3604480 | tf_op jit(solution)/shard_map/all_gather | solution.py:234
  45.1 66.8 %collective-permute-start.10 = (bf16[256,2048]{1,0:T(8,128)(2,1)}, bf16[256,2048]{1,0:T(8,128)(2,1)}, u32[]{:S(2)}, u32[]{:S(2)}) collective-permute-start(bf16[256,2048]{1,0:T(8,128)(2,1)} %all-gather.14.cloned.1.call-done), channel_id=1, source_target_pairs={{0,16},{4,20},{8,24},{12,28},{16,0},{20,4},{24,8},{28,12},{1,17},{... | collective-permute-start | bytes 3145736 | tf_op jit(solution)/shard_map/ppermute | solution.py:29
  106.0 104.2 %collective-permute-start.5 = (bf16[2048,768]{1,0:T(8,128)(2,1)}, bf16[2048,768]{1,0:T(8,128)(2,1)}, u32[]{:S(2)}, u32[]{:S(2)}) collective-permute-start(bf16[2048,768]{1,0:T(8,128)(2,1)} %all-gather.12.cloned.1.call-done), channel_id=1, source_target_pairs={{0,8},{4,12},{8,0},{12,4},{16,24},{20,28},{24,16},{28,20},{1,9},{5... | collective-permute-start | bytes 9437192 | tf_op jit(solution)/shard_map/ppermute | solution.py:29
  113.0 74.2 %collective-permute-start.12 = (bf16[128,2048]{1,0:T(8,128)(2,1)S(1)}, bf16[128,2048]{1,0:T(8,128)(2,1)S(1)}, u32[]{:S(2)}, u32[]{:S(2)}) collective-permute-start(bf16[128,2048]{1,0:T(8,128)(2,1)S(1)} %slice.473), channel_id=1, source_target_pairs={{0,8},{4,12},{8,0},{12,4},{16,24},{20,28},{24,16},{28,20},{1,9},{5... | collective-permute-start | bytes 1572872 | tf_op jit(solution)/shard_map/ppermute | solution.py:29
  115.0 106.0 %collective-permute-start.6 = (bf16[2048,768]{1,0:T(8,128)(2,1)}, bf16[2048,768]{1,0:T(8,128)(2,1)}, u32[]{:S(2)}, u32[]{:S(2)}) collective-permute-start(bf16[2048,768]{1,0:T(8,128)(2,1)} %all-gather.12.cloned.1.call-done), channel_id=1, source_target_pairs={{0,16},{4,20},{8,24},{12,28},{16,0},{20,4},{24,8},{28,12},{1,17},{... | collective-permute-start | bytes 9437192 | tf_op jit(solution)/shard_map/ppermute | solution.py:29
  212.9 52.7 %collective-permute-start.7 = (bf16[1024,768]{1,0:T(8,128)(2,1)}, bf16[1024,768]{1,0:T(8,128)(2,1)}, u32[]{:S(2)}, u32[]{:S(2)}) collective-permute-start(bf16[1024,768]{1,0:T(8,128)(2,1)} %slice.463), channel_id=1, source_target_pairs={{0,16},{4,20},{8,24},{12,28},{16,0},{20,4},{24,8},{28,12},{1,17},{... | collective-permute-start | bytes 4718600 | tf_op jit(solution)/shard_map/ppermute | solution.py:29
  233.8 35.3 %collective-permute-start.8 = (bf16[1024,768]{1,0:T(8,128)(2,1)}, bf16[1024,768]{1,0:T(8,128)(2,1)}, u32[]{:S(2)}, u32[]{:S(2)}) collective-permute-start(bf16[1024,768]{1,0:T(8,128)(2,1)} %slice.464), channel_id=1, source_target_pairs={{0,8},{4,12},{8,0},{12,4},{16,24},{20,28},{24,16},{28,20},{1,9},{5... | collective-permute-start | bytes 4718600 | tf_op jit(solution)/shard_map/ppermute | solution.py:29
  383.7 364.2 %reduce-scatter.7.cloned.1.call-start = ((), (), s32[]{:S(2)}) async-start(), calls=%async_computation.12 | async-start | bytes 1310720 | tf_op jit(solution)/shard_map/reduce_scatter | solution.py:304
  539.3 209.3 %reduce-scatter.11.cloned.1.call-start = ((), (), s32[]{:S(2)}) async-start(), calls=%async_computation.17 | async-start | bytes 3604480 | tf_op jit(solution)/shard_map/reduce_scatter | solution.py:300
  547.1 248.2 %reduce-scatter.5.cloned.1.call-start = ((), (), s32[]{:S(2)}) async-start(), calls=%async_computation.8 | async-start | bytes 3932160 | tf_op jit(solution)/shard_map/reduce_scatter | solution.py:306
  623.0 37.6 %collective-permute-start.41 = (bf16[1024,768]{1,0:T(8,128)(2,1)}, bf16[1024,768]{1,0:T(8,128)(2,1)}, u32[]{:S(2)}, u32[]{:S(2)}) collective-permute-start(bf16[1024,768]{1,0:T(8,128)(2,1)} %get-tuple-element.55), channel_id=1, source_target_pairs={{0,16},{4,20},{8,24},{12,28},{16,0},{20,4},{24,8},{28,12},{1,17},{... | collective-permute-start | bytes 4718600 | tf_op jit(solution)/shard_map/ppermute | solution.py:29
  624.5 40.8 %collective-permute-start.43 = (bf16[1024,768]{1,0:T(8,128)(2,1)}, bf16[1024,768]{1,0:T(8,128)(2,1)}, u32[]{:S(2)}, u32[]{:S(2)}) collective-permute-start(bf16[1024,768]{1,0:T(8,128)(2,1)} %get-tuple-element.54), channel_id=1, source_target_pairs={{0,8},{4,12},{8,0},{12,4},{16,24},{20,28},{24,16},{28,20},{1,9},{5... | collective-permute-start | bytes 4718600 | tf_op jit(solution)/shard_map/ppermute | solution.py:29
  640.3 55.5 %collective-permute-start.40 = (bf16[1024,768]{1,0:T(8,128)(2,1)}, bf16[1024,768]{1,0:T(8,128)(2,1)}, u32[]{:S(2)}, u32[]{:S(2)}) collective-permute-start(bf16[1024,768]{1,0:T(8,128)(2,1)} %slice.523), channel_id=1, source_target_pairs={{0,8},{4,12},{8,0},{12,4},{16,24},{20,28},{24,16},{28,20},{1,9},{5... | collective-permute-start | bytes 4718600 | tf_op jit(solution)/shard_map/ppermute | solution.py:29
  650.0 45.8 %collective-permute-start.45 = (bf16[1024,768]{1,0:T(8,128)(2,1)}, bf16[1024,768]{1,0:T(8,128)(2,1)}, u32[]{:S(2)}, u32[]{:S(2)}) collective-permute-start(bf16[1024,768]{1,0:T(8,128)(2,1)} %slice.528), channel_id=1, source_target_pairs={{0,16},{4,20},{8,24},{12,28},{16,0},{20,4},{24,8},{28,12},{1,17},{... | collective-permute-start | bytes 4718600 | tf_op jit(solution)/shard_map/ppermute | solution.py:29
  663.7 63.7 %collective-permute-start.42 = (bf16[1024,768]{1,0:T(8,128)(2,1)}, bf16[1024,768]{1,0:T(8,128)(2,1)}, u32[]{:S(2)}, u32[]{:S(2)}) collective-permute-start(bf16[1024,768]{1,0:T(8,128)(2,1)} %add_convert_fusion.5), channel_id=1, source_target_pairs={{0,8},{4,12},{8,0},{12,4},{16,24},{20,28},{24,16},{28,20},{1,9},{5... | collective-permute-start | bytes 4718600 | tf_op jit(solution)/shard_map/ppermute | solution.py:29
  668.4 59.1 %collective-permute-start.44 = (bf16[1024,768]{1,0:T(8,128)(2,1)}, bf16[1024,768]{1,0:T(8,128)(2,1)}, u32[]{:S(2)}, u32[]{:S(2)}) collective-permute-start(bf16[1024,768]{1,0:T(8,128)(2,1)} %add_convert_fusion.4), channel_id=1, source_target_pairs={{0,16},{4,20},{8,24},{12,28},{16,0},{20,4},{24,8},{28,12},{1,17},{... | collective-permute-start | bytes 4718600 | tf_op jit(solution)/shard_map/ppermute | solution.py:29
  736.8 163.8 %reduce-scatter.9.cloned.1.call-start = ((), (), s32[]{:S(2)}) async-start(), calls=%async_computation.14 | async-start | bytes 7208960 | tf_op jit(solution)/shard_map/reduce_scatter | solution.py:299
  747.8 299.1 %all-gather.26.cloned.1.call-start = ((), (), s32[]{:S(2)}) async-start(), calls=%async_computation.13 | async-start | bytes 2359296 | tf_op jit(solution)/shard_map/all_gather | solution.py:297
  748.6 302.6 %all-gather.32.cloned.1.call-start = ((), (), s32[]{:S(2)}) async-start(), calls=%async_computation.18 | async-start | bytes 6488064 | tf_op jit(solution)/shard_map/all_gather | solution.py:297
  749.1 310.7 %all-gather.20.cloned.1.call-start = ((), (), s32[]{:S(2)}) async-start(), calls=%async_computation.9 | async-start | bytes 2359296 | tf_op jit(solution)/shard_map/all_gather | solution.py:297
  797.3 266.8 %all-gather.22.cloned.1.call-start = ((), (), s32[]{:S(2)}) async-start(), calls=%async_computation.10 | async-start | bytes 2359296 | tf_op jit(solution)/shard_map/all_gather | solution.py:297
  797.9 283.6 %all-gather.24.cloned.1.call-start = ((), (), s32[]{:S(2)}) async-start(), calls=%async_computation.11 | async-start | bytes 2359296 | tf_op jit(solution)/shard_map/all_gather | solution.py:297
  798.7 328.1 %all-gather.28.cloned.1.call-start = ((), (), s32[]{:S(2)}) async-start(), calls=%async_computation.15 | async-start | bytes 6488064 | tf_op jit(solution)/shard_map/all_gather | solution.py:297
  903.6 268.4 %all-gather.30.cloned.1.call-start = ((), (), s32[]{:S(2)}) async-start(), calls=%async_computation.16 | async-start | bytes 6488064 | tf_op jit(solution)/shard_map/all_gather | solution.py:297
  914.1 37.1 %collective-permute-start.19 = (bf16[512,2048]{1,0:T(8,128)(2,1)}, bf16[512,2048]{1,0:T(8,128)(2,1)}, u32[]{:S(2)}, u32[]{:S(2)}) collective-permute-start(bf16[512,2048]{1,0:T(8,128)(2,1)} %slice.482), channel_id=1, source_target_pairs={{0,4},{4,0},{8,12},{12,8},{16,20},{20,16},{24,28},{28,24},{1,5},{5... | collective-permute-start | bytes 6291464 | tf_op jit(solution)/shard_map/ppermute | solution.py:29
  951.0 44.8 %collective-permute-start.39 = (bf16[512,2048]{1,0:T(8,128)(2,1)}, bf16[512,2048]{1,0:T(8,128)(2,1)}, u32[]{:S(2)}, u32[]{:S(2)}) collective-permute-start(bf16[512,2048]{1,0:T(8,128)(2,1)} %slice.618), channel_id=1, source_target_pairs={{0,4},{4,0},{8,12},{12,8},{16,20},{20,16},{24,28},{28,24},{1,5},{5... | collective-permute-start | bytes 6291464 | tf_op jit(solution)/shard_map/ppermute | solution.py:29
  (174 other events, 2055.3 us)
Sparse Core Ops, SparseCore 0:
  10.2 30.6 all-gather.13
  43.0 62.9 all-gather.11
  107.6 105.3 all-gather.15
  383.8 57.9 all-gather.17
  539.5 25.8 reduce-scatter.6
  567.6 54.8 reduce-scatter.10
  736.9 58.3 reduce-scatter.4
  798.3 102.2 reduce-scatter.8
  902.6 28.3 all-gather.25
  933.0 56.7 all-gather.31
  991.8 29.1 all-gather.19
  1022.8 28.3 all-gather.21
  1053.3 28.1 all-gather.23
  1083.4 43.3 all-gather.27
  1128.6 43.3 all-gather.29
where the time goes:
time: 1190 us
  waiting for transfers between devices  592 us (50%)
  matrix products  222 us (19%)
  local copies, waits for them, and re-layouts  180 us (15%)
  other arithmetic  85.9 us (7%)
  starting transfers between devices  52.3 us (4%)
  blocking collectives  39.9 us (3%)
  between operations  16.3 us (1%)
    ppermute x49, waiting for transfers between devices, swap(): return lax.ppermute(value, 'rep', [(i, i ^ bit) for i in range(size)])  238 us
    reduce_scatter x1, waiting for transfers between devices, per_device(): lax.psum_scatter(grad_gate_up, 'shard', scatter_dimension=0, tiled=True)  102 us
    all_gather x7, waiting for transfers between devices, spread(): return lax.all_gather(value, 'rep', axis=axis, tiled=True).astype(F32)  90.6 us
    dot_general x9, matrix products, mm_tn(): lax.dot_general(left, right, (((0,), (0,)), ((), ())), preferred_element_...  59.7 us
    dot_general x7, matrix products, mm_nt(): lax.dot_general(left, right, (((1,), (1,)), ((), ())), preferred_element_...  59.5 us
    all_gather x1, waiting for transfers between devices, per_device(): own_qkv = lax.all_gather(own_qkv, 'shard', axis=0, tiled=True)  57.4 us
    dot_general x9, matrix products, mm(): return jnp.dot(left, right, preferred_element_type=F32)  54.5 us
    unnamed x308, local copies, waits for them, and re-layouts  49.1 us
  transfers between devices with their start and end apart: 67, of which 40 were waited for; matrix products, arithmetic and copies ran while one was open for 36% of the time, Pallas kernels for 0%

commit v1 on v0

--- a/solution.py
+++ b/solution.py
@@ -311,7 +311,9 @@
     grad_query, grad_key, grad_value = (
         spread(sum_qkv[:, i * block : (i + 1) * block], 1) for i in range(3)
     )
-    gain_grads = lax.psum(jnp.stack([grad_gain_one, grad_gain_two]), ("rep", "shard"))
+    part = jnp.stack([grad_gain_one, grad_gain_two])
+    pieces = lax.all_gather(part, ("rep", "shard"))
+    gain_grads = jnp.sum(pieces, axis=0)
     own = gain_attn.shape[0]
     gain_grads = lax.dynamic_slice_in_dim(gain_grads, lax.axis_index("shard") * own, own, 1)
     return (

time: 1190 us -> 1190 us (level)
  waiting for transfers between devices: 592 us -> 560 us
  blocking collectives: 39.9 us -> 71.6 us
    all_gather x0 -> x1, blocking collectives: none -> 71.6 us  [per_device(): pieces = lax.all_gather(part, ('rep', 'shard'))]
    psum x1 -> x0, blocking collectives: 39.9 us -> none  [per_device(): lax.psum(jnp.stack([grad_gain_one, grad_gain_two]), ('rep', 'shard'))]
    all_gather x7, waiting for transfers between devices: 90.6 us -> 58.7 us  [spread(): return lax.all_gather(value, 'rep', axis=axis, tiled=True).astype(F32)]
  transfers between devices with their start and end apart: 67 -> 67, of which waited for: 40 -> 39; matrix products, arithmetic and copies ran while one was open for 36% -> 36% of each run, Pallas kernels for 0% -> 0%
where the time goes in v1:
time: 1190 us
  waiting for transfers between devices  560 us (47%)
  matrix products  222 us (19%)
  local copies, waits for them, and re-layouts  180 us (15%)
  other arithmetic  86 us (7%)
  blocking collectives  71.6 us (6%)
  starting transfers between devices  52.3 us (4%)
  between operations  16.3 us (1%)
    ppermute x49, waiting for transfers between devices, swap(): return lax.ppermute(value, 'rep', [(i, i ^ bit) for i in range(size)])  238 us
    reduce_scatter x1, waiting for transfers between devices, per_device(): lax.psum_scatter(grad_gate_up, 'shard', scatter_dimension=0, tiled=True)  102 us
    all_gather x1, blocking collectives, per_device(): pieces = lax.all_gather(part, ('rep', 'shard'))  71.6 us
    dot_general x9, matrix products, mm_tn(): lax.dot_general(left, right, (((0,), (0,)), ((), ())), preferred_element_...  59.7 us
    dot_general x7, matrix products, mm_nt(): lax.dot_general(left, right, (((1,), (1,)), ((), ())), preferred_element_...  59.5 us
    all_gather x7, waiting for transfers between devices, spread(): return lax.all_gather(value, 'rep', axis=axis, tiled=True).astype(F32)  58.7 us
    all_gather x1, waiting for transfers between devices, per_device(): own_qkv = lax.all_gather(own_qkv, 'shard', axis=0, tiled=True)  57.4 us
    dot_general x9, matrix products, mm(): return jnp.dot(left, right, preferred_element_type=F32)  54.5 us
  transfers between devices with their start and end apart: 67, of which 39 were waited for; matrix products, arithmetic and copies ran while one was open for 36% of the time, Pallas kernels for 0%

profile of v1, /device:TPU:0, one launch (start us, length us, event | category | flops | bytes accessed | tf_op | source)
XLA Modules:
  0.0 1188.0 jit_solution(11623226232861256016)
XLA Ops:
  25.8 15.1 %all-gather.16.cloned.1.call-done = bf16[256,2048]{1,0:T(8,128)(2,1)} async-done(((bf16[256,512]{1,0:T(8,128)(2,1)}), bf16[256,2048]{1,0:T(8,128)(2,1)}) %all-gather.16.cloned.1.call-update) | async-done | bytes 1048592 | tf_op jit(solution)/shard_map/all_gather | solution.py:229
  48.7 57.4 %all-gather.14.cloned.1.call-done = bf16[2048,768]{1,0:T(8,128)(2,1)} async-done(((bf16[512,768]{1,0:T(8,128)(2,1)}), bf16[2048,768]{1,0:T(8,128)(2,1)}) %all-gather.14.cloned.1.call-update) | async-done | bytes 3145744 | tf_op jit(solution)/shard_map/all_gather | solution.py:228
  124.0 63.3 %collective-permute-done.12 = bf16[128,2048]{1,0:T(8,128)(2,1)S(1)} collective-permute-done((bf16[128,2048]{1,0:T(8,128)(2,1)S(1)}, bf16[128,2048]{1,0:T(8,128)(2,1)S(1)}, u32[]{:S(2)}, u32[]{:S(2)}) %collective-permute-start.12) | collective-permute-done | bytes 524320 | tf_op jit(solution)/shard_map/ppermute | solution.py:29
  221.0 8.6 fusion.149
  292.3 7.5 subtract_convert_fusion.9
  342.6 11.5 collective-permute-done.26
  364.9 8.4 collective-permute-done.14
  389.3 12.3 %fusion.178 = f32[1024,1408]{1,0:T(8,128)} fusion(bf16[1024,2048]{1,0:T(8,128)(2,1)} %constant_dynamic-update-slice_fusion.20, bf16[2048,1408]{1,0:T(8,128)(2,1)} %all-gather.18.cloned.1.call-done), kind=kOutput, calls=%fused_computation.378 | convolution fusion | flops 5905580032 | bytes 15728640 | tf_op jit(solution)/shard_map/dot_general | solution.py:16
  401.6 40.2 %all-gather.20.cloned.1.call-done = bf16[704,2048]{1,0:T(8,128)(2,1)} async-done(((bf16[704,512]{1,0:T(8,128)(2,1)}), bf16[704,2048]{1,0:T(8,128)(2,1)}) %all-gather.20.cloned.1.call-update) | async-done | bytes 2883600 | tf_op jit(solution)/shard_map/all_gather | solution.py:234
  441.8 10.3 multiply_convert_fusion.7
  505.1 10.7 collective-permute-done.49
  527.7 9.9 collective-permute-done.48
  539.5 7.6 convolution_convert_fusion.8
  626.2 8.0 convolution_convert_fusion.6
  650.6 10.1 collective-permute-done.41
  673.1 22.7 %collective-permute-done.40 = bf16[1024,768]{1,0:T(8,128)(2,1)} collective-permute-done((bf16[1024,768]{1,0:T(8,128)(2,1)}, bf16[1024,768]{1,0:T(8,128)(2,1)}, u32[]{:S(2)}, u32[]{:S(2)}) %collective-permute-start.40) | collective-permute-done | bytes 1572896 | tf_op jit(solution)/shard_map/ppermute | solution.py:29
  695.8 31.6 %collective-permute-done.42 = bf16[1024,768]{1,0:T(8,128)(2,1)} collective-permute-done((bf16[1024,768]{1,0:T(8,128)(2,1)}, bf16[1024,768]{1,0:T(8,128)(2,1)}, u32[]{:S(2)}, u32[]{:S(2)}) %collective-permute-start.42) | collective-permute-done | bytes 1572896 | tf_op jit(solution)/shard_map/ppermute | solution.py:29
  727.4 9.3 add_convert_fusion
  736.9 10.9 convolution_convert_fusion
  749.2 46.1 %reduce-scatter.5.cloned.1.call-done = bf16[512,768]{1,0:T(8,128)(2,1)} async-done(((bf16[2048,768]{1,0:T(8,128)(2,1)}), bf16[512,768]{1,0:T(8,128)(2,1)}) %reduce-scatter.5.cloned.1.call-update) | async-done | bytes 786448 | tf_op jit(solution)/shard_map/reduce_scatter | solution.py:306
  798.7 101.9 %reduce-scatter.9.cloned.1.call-done = bf16[512,1408]{1,0:T(8,128)(2,1)} async-done(((bf16[2048,1408]{1,0:T(8,128)(2,1)}), bf16[512,1408]{1,0:T(8,128)(2,1)}) %reduce-scatter.9.cloned.1.call-update) | async-done | bytes 1441808 | tf_op jit(solution)/shard_map/reduce_scatter | solution.py:299
  914.4 7.8 fusion.181
  922.2 7.7 fusion.179
  929.9 7.7 fusion.180
  937.6 11.8 add_add_fusion
  962.2 10.7 collective-permute-done.23
  1000.2 71.6 %all-gather.1 = f32[32,2,2048]{2,1,0:T(2,128)S(1)} all-gather(f32[1,2,2048]{2,1,0:T(2,128)S(1)} %maximum_bitcast_fusion), channel_id=2, replica_groups=mesh['rep'=8,'shard'=4] {'rep','shard'}, dimensions={0}, use_global_device_ids=true | all-gather | bytes 540672 | tf_op jit(solution)/shard_map/all_gather | solution.py:315
  1082.9 8.7 convert_element_type.490
  1104.2 22.5 %all-gather.30.cloned.1.call-done = bf16[512,5632]{0,1:T(8,128)(2,1)} async-done(((bf16[512,704]{0,1:T(8,128)(2,1)}), bf16[512,5632]{0,1:T(8,128)(2,1)}) %all-gather.30.cloned.1.call-update) | async-done | bytes 5767184 | tf_op jit(solution)/shard_map/all_gather | solution.py:297
  1126.7 9.1 copy.333
  1135.8 36.2 %all-gather.32.cloned.1.call-done = bf16[512,5632]{0,1:T(8,128)(2,1)} async-done(((bf16[512,704]{0,1:T(8,128)(2,1)}), bf16[512,5632]{0,1:T(8,128)(2,1)}) %all-gather.32.cloned.1.call-update) | async-done | bytes 5767184 | tf_op jit(solution)/shard_map/all_gather | solution.py:297
  1172.0 9.2 copy.334
  (634 shorter events, 465.4 us)
Async XLA Ops:
  7.2 33.6 %all-gather.16.cloned.1.call-start = ((), (), s32[]{:S(2)}) async-start(), calls=%async_computation.5 | async-start | bytes 1310720 | tf_op jit(solution)/shard_map/all_gather | solution.py:229
  9.5 96.5 %all-gather.14.cloned.1.call-start = ((), (), s32[]{:S(2)}) async-start(), calls=%async_computation.4 | async-start | bytes 3932160 | tf_op jit(solution)/shard_map/all_gather | solution.py:228
  12.7 376.6 %all-gather.18.cloned.1.call-start = ((), (), s32[]{:S(2)}) async-start(), calls=%async_computation.6 | async-start | bytes 7208960 | tf_op jit(solution)/shard_map/all_gather | solution.py:233
  18.9 88.6 %collective-permute-start.4 = (s32[1,512]{1,0:T(1,128)S(1)}, s32[1,512]{1,0:T(1,128)S(1)}, u32[]{:S(2)}, u32[]{:S(2)}) collective-permute-start(s32[1,512]{1,0:T(1,128)S(1)} %copy-done.131), channel_id=1, source_target_pairs={{0,4},{4,0},{8,12},{12,8},{16,20},{20,16},{24,28},{28,24},{1,5},{5... | collective-permute-start | bytes 6152 | tf_op jit(solution)/shard_map/ppermute | solution.py:29
  25.4 164.0 %collective-permute-start.3 = (bf16[512,2048]{1,0:T(8,128)(2,1)}, bf16[512,2048]{1,0:T(8,128)(2,1)}, u32[]{:S(2)}, u32[]{:S(2)}) collective-permute-start(bf16[512,2048]{1,0:T(8,128)(2,1)} %fusion.2), channel_id=1, source_target_pairs={{0,4},{4,0},{8,12},{12,8},{16,20},{20,16},{24,28},{28,24},{1,5},{5... | collective-permute-start | bytes 6291464 | tf_op jit(solution)/shard_map/ppermute | solution.py:29
  40.9 67.1 %collective-permute-start.9 = (bf16[256,2048]{1,0:T(8,128)(2,1)}, bf16[256,2048]{1,0:T(8,128)(2,1)}, u32[]{:S(2)}, u32[]{:S(2)}) collective-permute-start(bf16[256,2048]{1,0:T(8,128)(2,1)} %all-gather.16.cloned.1.call-done), channel_id=1, source_target_pairs={{0,8},{4,12},{8,0},{12,4},{16,24},{20,28},{24,16},{28,20},{1,9},{5... | collective-permute-start | bytes 3145736 | tf_op jit(solution)/shard_map/ppermute | solution.py:29
  45.0 396.7 %all-gather.20.cloned.1.call-start = ((), (), s32[]{:S(2)}) async-start(), calls=%async_computation.7 | async-start | bytes 3604480 | tf_op jit(solution)/shard_map/all_gather | solution.py:234
  45.1 66.8 %collective-permute-start.10 = (bf16[256,2048]{1,0:T(8,128)(2,1)}, bf16[256,2048]{1,0:T(8,128)(2,1)}, u32[]{:S(2)}, u32[]{:S(2)}) collective-permute-start(bf16[256,2048]{1,0:T(8,128)(2,1)} %all-gather.16.cloned.1.call-done), channel_id=1, source_target_pairs={{0,16},{4,20},{8,24},{12,28},{16,0},{20,4},{24,8},{28,12},{1,17},{... | collective-permute-start | bytes 3145736 | tf_op jit(solution)/shard_map/ppermute | solution.py:29
  106.0 104.2 %collective-permute-start.5 = (bf16[2048,768]{1,0:T(8,128)(2,1)}, bf16[2048,768]{1,0:T(8,128)(2,1)}, u32[]{:S(2)}, u32[]{:S(2)}) collective-permute-start(bf16[2048,768]{1,0:T(8,128)(2,1)} %all-gather.14.cloned.1.call-done), channel_id=1, source_target_pairs={{0,8},{4,12},{8,0},{12,4},{16,24},{20,28},{24,16},{28,20},{1,9},{5... | collective-permute-start | bytes 9437192 | tf_op jit(solution)/shard_map/ppermute | solution.py:29
  113.0 74.2 %collective-permute-start.12 = (bf16[128,2048]{1,0:T(8,128)(2,1)S(1)}, bf16[128,2048]{1,0:T(8,128)(2,1)S(1)}, u32[]{:S(2)}, u32[]{:S(2)}) collective-permute-start(bf16[128,2048]{1,0:T(8,128)(2,1)S(1)} %slice.473), channel_id=1, source_target_pairs={{0,8},{4,12},{8,0},{12,4},{16,24},{20,28},{24,16},{28,20},{1,9},{5... | collective-permute-start | bytes 1572872 | tf_op jit(solution)/shard_map/ppermute | solution.py:29
  115.0 106.0 %collective-permute-start.6 = (bf16[2048,768]{1,0:T(8,128)(2,1)}, bf16[2048,768]{1,0:T(8,128)(2,1)}, u32[]{:S(2)}, u32[]{:S(2)}) collective-permute-start(bf16[2048,768]{1,0:T(8,128)(2,1)} %all-gather.14.cloned.1.call-done), channel_id=1, source_target_pairs={{0,16},{4,20},{8,24},{12,28},{16,0},{20,4},{24,8},{28,12},{1,17},{... | collective-permute-start | bytes 9437192 | tf_op jit(solution)/shard_map/ppermute | solution.py:29
  212.9 52.7 %collective-permute-start.7 = (bf16[1024,768]{1,0:T(8,128)(2,1)}, bf16[1024,768]{1,0:T(8,128)(2,1)}, u32[]{:S(2)}, u32[]{:S(2)}) collective-permute-start(bf16[1024,768]{1,0:T(8,128)(2,1)} %slice.463), channel_id=1, source_target_pairs={{0,16},{4,20},{8,24},{12,28},{16,0},{20,4},{24,8},{28,12},{1,17},{... | collective-permute-start | bytes 4718600 | tf_op jit(solution)/shard_map/ppermute | solution.py:29
  233.8 35.3 %collective-permute-start.8 = (bf16[1024,768]{1,0:T(8,128)(2,1)}, bf16[1024,768]{1,0:T(8,128)(2,1)}, u32[]{:S(2)}, u32[]{:S(2)}) collective-permute-start(bf16[1024,768]{1,0:T(8,128)(2,1)} %slice.464), channel_id=1, source_target_pairs={{0,8},{4,12},{8,0},{12,4},{16,24},{20,28},{24,16},{28,20},{1,9},{5... | collective-permute-start | bytes 4718600 | tf_op jit(solution)/shard_map/ppermute | solution.py:29
  383.7 364.2 %reduce-scatter.7.cloned.1.call-start = ((), (), s32[]{:S(2)}) async-start(), calls=%async_computation.12 | async-start | bytes 1310720 | tf_op jit(solution)/shard_map/reduce_scatter | solution.py:304
  539.3 209.3 %reduce-scatter.11.cloned.1.call-start = ((), (), s32[]{:S(2)}) async-start(), calls=%async_computation.17 | async-start | bytes 3604480 | tf_op jit(solution)/shard_map/reduce_scatter | solution.py:300
  547.1 248.2 %reduce-scatter.5.cloned.1.call-start = ((), (), s32[]{:S(2)}) async-start(), calls=%async_computation.8 | async-start | bytes 3932160 | tf_op jit(solution)/shard_map/reduce_scatter | solution.py:306
  623.0 37.6 %collective-permute-start.41 = (bf16[1024,768]{1,0:T(8,128)(2,1)}, bf16[1024,768]{1,0:T(8,128)(2,1)}, u32[]{:S(2)}, u32[]{:S(2)}) collective-permute-start(bf16[1024,768]{1,0:T(8,128)(2,1)} %get-tuple-element.55), channel_id=1, source_target_pairs={{0,16},{4,20},{8,24},{12,28},{16,0},{20,4},{24,8},{28,12},{1,17},{... | collective-permute-start | bytes 4718600 | tf_op jit(solution)/shard_map/ppermute | solution.py:29
  624.5 40.8 %collective-permute-start.43 = (bf16[1024,768]{1,0:T(8,128)(2,1)}, bf16[1024,768]{1,0:T(8,128)(2,1)}, u32[]{:S(2)}, u32[]{:S(2)}) collective-permute-start(bf16[1024,768]{1,0:T(8,128)(2,1)} %get-tuple-element.54), channel_id=1, source_target_pairs={{0,8},{4,12},{8,0},{12,4},{16,24},{20,28},{24,16},{28,20},{1,9},{5... | collective-permute-start | bytes 4718600 | tf_op jit(solution)/shard_map/ppermute | solution.py:29
  640.3 55.5 %collective-permute-start.40 = (bf16[1024,768]{1,0:T(8,128)(2,1)}, bf16[1024,768]{1,0:T(8,128)(2,1)}, u32[]{:S(2)}, u32[]{:S(2)}) collective-permute-start(bf16[1024,768]{1,0:T(8,128)(2,1)} %slice.523), channel_id=1, source_target_pairs={{0,8},{4,12},{8,0},{12,4},{16,24},{20,28},{24,16},{28,20},{1,9},{5... | collective-permute-start | bytes 4718600 | tf_op jit(solution)/shard_map/ppermute | solution.py:29
  650.0 45.8 %collective-permute-start.45 = (bf16[1024,768]{1,0:T(8,128)(2,1)}, bf16[1024,768]{1,0:T(8,128)(2,1)}, u32[]{:S(2)}, u32[]{:S(2)}) collective-permute-start(bf16[1024,768]{1,0:T(8,128)(2,1)} %slice.528), channel_id=1, source_target_pairs={{0,16},{4,20},{8,24},{12,28},{16,0},{20,4},{24,8},{28,12},{1,17},{... | collective-permute-start | bytes 4718600 | tf_op jit(solution)/shard_map/ppermute | solution.py:29
  663.7 63.7 %collective-permute-start.42 = (bf16[1024,768]{1,0:T(8,128)(2,1)}, bf16[1024,768]{1,0:T(8,128)(2,1)}, u32[]{:S(2)}, u32[]{:S(2)}) collective-permute-start(bf16[1024,768]{1,0:T(8,128)(2,1)} %add_convert_fusion.5), channel_id=1, source_target_pairs={{0,8},{4,12},{8,0},{12,4},{16,24},{20,28},{24,16},{28,20},{1,9},{5... | collective-permute-start | bytes 4718600 | tf_op jit(solution)/shard_map/ppermute | solution.py:29
  668.4 59.1 %collective-permute-start.44 = (bf16[1024,768]{1,0:T(8,128)(2,1)}, bf16[1024,768]{1,0:T(8,128)(2,1)}, u32[]{:S(2)}, u32[]{:S(2)}) collective-permute-start(bf16[1024,768]{1,0:T(8,128)(2,1)} %add_convert_fusion.4), channel_id=1, source_target_pairs={{0,16},{4,20},{8,24},{12,28},{16,0},{20,4},{24,8},{28,12},{1,17},{... | collective-permute-start | bytes 4718600 | tf_op jit(solution)/shard_map/ppermute | solution.py:29
  736.8 163.8 %reduce-scatter.9.cloned.1.call-start = ((), (), s32[]{:S(2)}) async-start(), calls=%async_computation.14 | async-start | bytes 7208960 | tf_op jit(solution)/shard_map/reduce_scatter | solution.py:299
  747.8 330.9 %all-gather.28.cloned.1.call-start = ((), (), s32[]{:S(2)}) async-start(), calls=%async_computation.13 | async-start | bytes 2359296 | tf_op jit(solution)/shard_map/all_gather | solution.py:297
  748.6 334.4 %all-gather.34.cloned.1.call-start = ((), (), s32[]{:S(2)}) async-start(), calls=%async_computation.18 | async-start | bytes 6488064 | tf_op jit(solution)/shard_map/all_gather | solution.py:297
  749.1 342.5 %all-gather.22.cloned.1.call-start = ((), (), s32[]{:S(2)}) async-start(), calls=%async_computation.9 | async-start | bytes 2359296 | tf_op jit(solution)/shard_map/all_gather | solution.py:297
  797.3 298.6 %all-gather.24.cloned.1.call-start = ((), (), s32[]{:S(2)}) async-start(), calls=%async_computation.10 | async-start | bytes 2359296 | tf_op jit(solution)/shard_map/all_gather | solution.py:297
  797.9 302.2 %all-gather.26.cloned.1.call-start = ((), (), s32[]{:S(2)}) async-start(), calls=%async_computation.11 | async-start | bytes 2359296 | tf_op jit(solution)/shard_map/all_gather | solution.py:297
  798.7 328.1 %all-gather.30.cloned.1.call-start = ((), (), s32[]{:S(2)}) async-start(), calls=%async_computation.15 | async-start | bytes 6488064 | tf_op jit(solution)/shard_map/all_gather | solution.py:297
  903.6 268.4 %all-gather.32.cloned.1.call-start = ((), (), s32[]{:S(2)}) async-start(), calls=%async_computation.16 | async-start | bytes 6488064 | tf_op jit(solution)/shard_map/all_gather | solution.py:297
  914.1 37.1 %collective-permute-start.19 = (bf16[512,2048]{1,0:T(8,128)(2,1)}, bf16[512,2048]{1,0:T(8,128)(2,1)}, u32[]{:S(2)}, u32[]{:S(2)}) collective-permute-start(bf16[512,2048]{1,0:T(8,128)(2,1)} %slice.482), channel_id=1, source_target_pairs={{0,4},{4,0},{8,12},{12,8},{16,20},{20,16},{24,28},{28,24},{1,5},{5... | collective-permute-start | bytes 6291464 | tf_op jit(solution)/shard_map/ppermute | solution.py:29
  951.0 44.8 %collective-permute-start.39 = (bf16[512,2048]{1,0:T(8,128)(2,1)}, bf16[512,2048]{1,0:T(8,128)(2,1)}, u32[]{:S(2)}, u32[]{:S(2)}) collective-permute-start(bf16[512,2048]{1,0:T(8,128)(2,1)} %slice.618), channel_id=1, source_target_pairs={{0,4},{4,0},{8,12},{12,8},{16,20},{20,16},{24,28},{28,24},{1,5},{5... | collective-permute-start | bytes 6291464 | tf_op jit(solution)/shard_map/ppermute | solution.py:29
  (174 other events, 2087.2 us)
Sparse Core Ops, SparseCore 0:
  10.2 30.6 all-gather.15
  43.0 62.9 all-gather.13
  107.6 105.3 all-gather.17
  383.8 57.9 all-gather.19
  539.5 25.8 reduce-scatter.6
  567.6 54.8 reduce-scatter.10
  736.9 58.3 reduce-scatter.4
  798.3 102.2 reduce-scatter.8
  902.6 28.3 all-gather.27
  933.0 56.7 all-gather.33
  991.8 28.9 all-gather.21
  1022.7 28.5 all-gather.23
  1053.3 28.1 all-gather.25
  1083.4 43.3 all-gather.29
  1128.6 43.3 all-gather.31
